TPU v7x, 512 devices: a whole 4x4x16 slice. The times are simulated.
512 devices in a mesh: grp: 64 (over z, x_lo, core), rep: 8 (over y, x_hi).
Axes of the slice: x: 4 (x_hi: 2, x_lo: 2; x = x_hi * 2 + x_lo), y: 4, z: 16, core: 2. Of those that a mesh axis runs over, the one named last changes fastest.
Arguments:
- adjoint: bfloat16 [1024, 512], P('grp'), may hold values from -6 to 6
- active: int32 [1024, 512], P('grp'), may hold values 0 or 1
- counts: int32 [1024, 65536], P('rep', 'grp'), may hold values from 0 to 3, as said below
- src_degree: int32 [1024], P('rep'), may hold values from 8 to 256
- dst_degree: int32 [65536], P('grp'), may hold values from 8 to 256
- inputs: bfloat16 [65536, 512], P(('grp', 'rep')), may hold values from -6 to 6
- weight: bfloat16 [512, 512], replicated, may hold values from -0.25 to 0.25
Outputs:
- grad_input: bfloat16 [65536, 512], P(('grp', 'rep'))
- grad_weight: float32 [512, 512], P('rep')
Inputs may be any that keep to these rules, and one draw needn't show every extreme that they name: Edge counts; within an aligned tile of 16 source rows by 1024 destination columns the share of nonzero entries ranges from none to all, differing from tile to tile.
All inputs are finite; a program needn't handle non-finite values. No bound on the sum of `active` on one device may be relied on, other than what follows from the above.
Results may differ from a plain program's by a relative error of at most 0.0057.
Values may be sent and summed in bfloat16 or wider, within the bound.
A program may use at most 64 MiB of HBM per device.

v0:
```python
import jax
import jax.numpy as jnp
from jax import lax
from jax.sharding import PartitionSpec as P


def spread(shard, axis, root):
    mine = lax.axis_index(axis) == root
    return lax.psum(jnp.where(mine, shard, jnp.zeros_like(shard)), axis)


def weight_term(row_inputs, values):
    high_part = values.astype(jnp.bfloat16)
    low_part = (values - high_part.astype(jnp.float32)).astype(jnp.bfloat16)
    upper = lax.dot_general(
        row_inputs, high_part, (((0,), (0,)), ((), ())), preferred_element_type=jnp.float32
    )
    lower = lax.dot_general(
        row_inputs, low_part, (((0,), (0,)), ((), ())), preferred_element_type=jnp.float32
    )
    return upper + lower


def body(adjoint, active, counts, src_degree, dst_degree, inputs, weight):
    masked = (adjoint.astype(jnp.float32) * active.astype(jnp.float32)).astype(jnp.bfloat16)
    src_scale = lax.rsqrt(src_degree.astype(jnp.float32))
    dst_scale = lax.rsqrt(dst_degree.astype(jnp.float32))
    src_rows = adjoint.shape[0]
    blocks = counts.shape[0] // src_rows
    replica = lax.axis_index("rep")

    def scaled_product(count_tile, row_scale, owner_rows, running):
        scaled_tile = (
            count_tile.astype(jnp.float32) * row_scale[:, None] * dst_scale[None, :]
        ).astype(jnp.bfloat16)
        return running + lax.dot_general(
            scaled_tile, owner_rows, (((0,), (0,)), ((), ())), preferred_element_type=jnp.float32
        )

    def apply_tile(block_index, running):
        owner_index = replica * blocks + block_index
        owner_rows = spread(masked, "grp", owner_index)
        start = block_index * src_rows
        count_tile = lax.dynamic_slice_in_dim(counts, start, src_rows, 0)
        row_scale = lax.dynamic_slice_in_dim(src_scale, start, src_rows, 0)
        return scaled_product(count_tile, row_scale, owner_rows, running)

    partial_value = lax.fori_loop(
        0, blocks, apply_tile, jnp.zeros((counts.shape[1], masked.shape[1]), jnp.float32)
    )
    grad_pre = lax.psum_scatter(partial_value, "rep", scatter_dimension=0, tiled=True)
    grad_input = lax.dot_general(
        grad_pre.astype(jnp.bfloat16),
        weight,
        (((1,), (1,)), ((), ())),
        preferred_element_type=jnp.float32,
    ).astype(jnp.bfloat16)
    vertex_total = inputs.shape[0] * lax.axis_size("grp") * lax.axis_size("rep")
    local_term = weight_term(inputs, grad_pre)
    whole_term = lax.psum(local_term, "grp")
    grad_weight = lax.psum_scatter(whole_term, "rep", scatter_dimension=0, tiled=True)
    return (grad_input, grad_weight / vertex_total)


def solution(mesh):
    in_specs = (
        P("grp", None),
        P("grp", None),
        P("rep", "grp"),
        P("rep"),
        P("grp"),
        P(("grp", "rep"), None),
        P(),
    )
    out_specs = (P(("grp", "rep"), None), P("rep", None))
    return jax.shard_map(body, mesh=mesh, in_specs=in_specs, out_specs=out_specs, check_vma=False)
```

profile of v0, /device:TPU:1, one launch (start us, length us, event | category | flops | bytes accessed | tf_op | source)
XLA Modules:
  0.0 2293.0 jit_solution(14087357009032355527)
XLA Ops:
  7.2 0.7 convert_rsqrt_fusion.1
  7.9 0.7 convert_rsqrt_fusion
  8.6 0.8 multiply_convert_fusion.2
  9.4 1680.2 %while.16 = (s32[]{:T(128)}, f32[1024,512]{1,0:T(8,128)S(1)}, s32[128,1024]{1,0:T(8,128)}, f32[128]{0:T(128)S(1)}, f32[1024]{0:T(1024)S(1)}, /*index=5*/s32[]{:T...) while((s32[]{:T(128)}, f32[1024,512]{1,0:T(8,128)S(1)}, ...), condition=%wide.region_2.3_spmd.clone, body=%wide.region_0.2_spmd.clone.sunk | while | flops 17907724 | bytes 4346299 | solution.py:48
  9.5 214.4 %psum.24 = bf16[16,512]{1,0:T(8,128)(2,1)S(1)} all-reduce(bf16[16,512]{1,0:T(8,128)(2,1)S(1)} %broadcast_select_fusion.2), channel_id=1, replica_groups=mesh['grp'=64,'rep'=8] {'grp'}, use_global_device_ids=true, to_apply=%region_1.1 | all-reduce | flops 8192 | bytes 32768 | tf_op jit(solution)/shard_map/while/body/eval_jaxpr/psum | solution.py:9
  223.9 1.6 select_add_fusion.2
  225.6 207.5 %psum.24 = bf16[16,512]{1,0:T(8,128)(2,1)S(1)} all-reduce(bf16[16,512]{1,0:T(8,128)(2,1)S(1)} %broadcast_select_fusion.2), channel_id=1, replica_groups=mesh['grp'=64,'rep'=8] {'grp'}, use_global_device_ids=true, to_apply=%region_1.1 | all-reduce | flops 8192 | bytes 32768 | tf_op jit(solution)/shard_map/while/body/eval_jaxpr/psum | solution.py:9
  433.1 1.5 select_add_fusion.2
  434.7 207.5 %psum.24 = bf16[16,512]{1,0:T(8,128)(2,1)S(1)} all-reduce(bf16[16,512]{1,0:T(8,128)(2,1)S(1)} %broadcast_select_fusion.2), channel_id=1, replica_groups=mesh['grp'=64,'rep'=8] {'grp'}, use_global_device_ids=true, to_apply=%region_1.1 | all-reduce | flops 8192 | bytes 32768 | tf_op jit(solution)/shard_map/while/body/eval_jaxpr/psum | solution.py:9
  642.2 1.6 select_add_fusion.2
  643.8 0.1 dynamic_slice.25
  643.9 207.5 %psum.24 = bf16[16,512]{1,0:T(8,128)(2,1)S(1)} all-reduce(bf16[16,512]{1,0:T(8,128)(2,1)S(1)} %broadcast_select_fusion.2), channel_id=1, replica_groups=mesh['grp'=64,'rep'=8] {'grp'}, use_global_device_ids=true, to_apply=%region_1.1 | all-reduce | flops 8192 | bytes 32768 | tf_op jit(solution)/shard_map/while/body/eval_jaxpr/psum | solution.py:9
  851.4 1.5 select_add_fusion.2
  853.1 207.5 %psum.24 = bf16[16,512]{1,0:T(8,128)(2,1)S(1)} all-reduce(bf16[16,512]{1,0:T(8,128)(2,1)S(1)} %broadcast_select_fusion.2), channel_id=1, replica_groups=mesh['grp'=64,'rep'=8] {'grp'}, use_global_device_ids=true, to_apply=%region_1.1 | all-reduce | flops 8192 | bytes 32768 | tf_op jit(solution)/shard_map/while/body/eval_jaxpr/psum | solution.py:9
  1060.6 1.6 select_add_fusion.2
  1062.2 207.5 %psum.24 = bf16[16,512]{1,0:T(8,128)(2,1)S(1)} all-reduce(bf16[16,512]{1,0:T(8,128)(2,1)S(1)} %broadcast_select_fusion.2), channel_id=1, replica_groups=mesh['grp'=64,'rep'=8] {'grp'}, use_global_device_ids=true, to_apply=%region_1.1 | all-reduce | flops 8192 | bytes 32768 | tf_op jit(solution)/shard_map/while/body/eval_jaxpr/psum | solution.py:9
  1269.7 1.5 select_add_fusion.2
  1271.4 207.5 %psum.24 = bf16[16,512]{1,0:T(8,128)(2,1)S(1)} all-reduce(bf16[16,512]{1,0:T(8,128)(2,1)S(1)} %broadcast_select_fusion.2), channel_id=1, replica_groups=mesh['grp'=64,'rep'=8] {'grp'}, use_global_device_ids=true, to_apply=%region_1.1 | all-reduce | flops 8192 | bytes 32768 | tf_op jit(solution)/shard_map/while/body/eval_jaxpr/psum | solution.py:9
  1478.9 1.6 select_add_fusion.2
  1480.6 207.5 %psum.24 = bf16[16,512]{1,0:T(8,128)(2,1)S(1)} all-reduce(bf16[16,512]{1,0:T(8,128)(2,1)S(1)} %broadcast_select_fusion.2), channel_id=1, replica_groups=mesh['grp'=64,'rep'=8] {'grp'}, use_global_device_ids=true, to_apply=%region_1.1 | all-reduce | flops 8192 | bytes 32768 | tf_op jit(solution)/shard_map/while/body/eval_jaxpr/psum | solution.py:9
  1688.1 1.5 select_add_fusion.2
  1689.7 1.3 copy-done.1
  1691.1 89.1 %reduce-scatter.5.cloned.1.call-done = f32[128,512]{1,0:T(8,128)} async-done(((f32[1024,512]{1,0:T(8,128)}), f32[128,512]{1,0:T(8,128)}) %reduce-scatter.5.cloned.1.call-update) | async-done | bytes 262160 | tf_op jit(solution)/shard_map/reduce_scatter | solution.py:51
  1780.1 1.3 fusion.5
  1781.4 1.4 fusion.3
  1782.8 1.3 copy.11
  1784.1 86.7 %reduce-scatter.7.cloned.1.call-done = f32[64,512]{1,0:T(8,128)} async-done(((f32[512,512]{1,0:T(8,128)}), f32[64,512]{1,0:T(8,128)}) %reduce-scatter.7.cloned.1.call-update) | async-done | bytes 131088
  1870.9 1.7 copy.12
  1872.6 1.0 convolution_convert_fusion
  1873.6 411.2 %all-reduce.2.cloned.1.call-done = f32[64,512]{0,1:T(8,128)} async-done(((f32[64,512]{0,1:T(8,128)}), f32[64,512]{0,1:T(8,128)}) %all-reduce.2.cloned.1.call-update) | async-done | bytes 131088 | tf_op jit(solution)/shard_map/psum | solution.py:60
  2284.8 1.0 broadcast_multiply_fusion
  2285.7 0.8 copy.10
  (29 shorter events, 0.8 us)
Async XLA Ops:
  7.2 1865.5 %copy-start = (bf16[512,512]{1,0:T(8,128)(2,1)S(1)}, bf16[512,512]{1,0:T(8,128)(2,1)}, u32[]{:S(2)}) copy-start(bf16[512,512]{1,0:T(8,128)(2,1)} %param.15) | copy-start | bytes 1572868
  7.2 1772.9 %reduce-scatter.5.cloned.1.call-start = ((), (), s32[]{:S(2)}) async-start(), calls=%async_computation.2 | async-start | bytes 2359296 | tf_op jit(solution)/shard_map/reduce_scatter | solution.py:51
  1689.6 1.3 copy-start.1
  1689.7 90.5 %copy-start.3 = (bf16[128,512]{1,0:T(8,128)(2,1)S(1)}, bf16[128,512]{1,0:T(8,128)(2,1)}, u32[]{:S(2)}) copy-start(bf16[128,512]{1,0:T(8,128)(2,1)} %param.14) | copy-start | bytes 393220
  1691.0 179.9 %reduce-scatter.7.cloned.1.call-start = ((), (), s32[]{:S(2)}) async-start(), calls=%async_computation.4 | async-start | bytes 1179648
  1782.7 89.9 %copy-start.2 = (f32[128,512]{1,0:T(8,128)S(1)}, f32[128,512]{1,0:T(8,128)}, u32[]{:S(2)}) copy-start(f32[128,512]{1,0:T(8,128)} %reduce-scatter.5.cloned.1.call-done) | copy-start | bytes 786436
  1784.1 500.7 %all-reduce.2.cloned.1.call-start = ((), (), s32[]{:S(2)}) async-start(), calls=%async_computation.3 | async-start | bytes 524288 | tf_op jit(solution)/shard_map/psum | solution.py:60
Sparse Core Ops, SparseCore 0:
  1691.1 88.9 reduce-scatter.4
  1784.6 86.2 reduce-scatter.6
  1873.8 410.9 all-reduce.1
where the time goes:
time: 2290 us
  blocking collectives  1670 us (73%)
  waiting for transfers between devices  587 us (26%)
    psum x8, blocking collectives, spread(): return lax.psum(jnp.where(mine, shard, jnp.zeros_like(shard)), axis)  1670 us
    psum x1, waiting for transfers between devices, body(): whole_term = lax.psum(local_term, 'grp')  411 us
    reduce_scatter x1, waiting for transfers between devices, body(): lax.psum_scatter(partial_value, 'rep', scatter_dimension=0, tiled=True)  89.1 us
    unnamed x4, waiting for transfers between devices  86.8 us
  transfers between devices with their start and end apart: 3, of which 3 were waited for; matrix products, arithmetic and copies ran while one was open for 0% of the time, Pallas kernels for 0%

commit v1 on v0

--- a/solution.py
+++ b/solution.py
@@ -6,7 +6,7 @@
 
 def spread(shard, axis, root):
     mine = lax.axis_index(axis) == root
-    return lax.psum(jnp.where(mine, shard, jnp.zeros_like(shard)), axis)
+    return jnp.sum(lax.all_gather(jnp.where(mine, shard, jnp.zeros_like(shard)), axis), axis=0)
 
 
 def weight_term(row_inputs, values):

time: 2290 us -> 1620 us (0.71)
  blocking collectives: 1670 us -> 0 us
  waiting for transfers between devices: 587 us -> 1560 us
    psum x8 -> x0, blocking collectives: 1670 us -> none  [spread(): return lax.psum(jnp.where(mine, shard, jnp.zeros_like(shard)), axis)]
    all_gather x0 -> x8, waiting for transfers between devices: none -> 972 us  [spread(): lax.all_gather(jnp.where(mine, shard, jnp.zeros_like(shard)), axis)]
  transfers between devices with their start and end apart: 3 -> 11, of which waited for: 3 -> 11; matrix products, arithmetic and copies ran while one was open for 0% -> 0% of each run, Pallas kernels for 0% -> 0%
where the time goes in v1:
time: 1620 us
  waiting for transfers between devices  1560 us (96%)
  other arithmetic  19.3 us (1%)
    all_gather x8, waiting for transfers between devices, spread(): lax.all_gather(jnp.where(mine, shard, jnp.zeros_like(shard)), axis)  972 us
    psum x1, waiting for transfers between devices, body(): whole_term = lax.psum(local_term, 'grp')  411 us
    reduce_scatter x1, waiting for transfers between devices, body(): lax.psum_scatter(partial_value, 'rep', scatter_dimension=0, tiled=True)  89.9 us
    unnamed x4, waiting for transfers between devices  86.8 us
  transfers between devices with their start and end apart: 11, of which 11 were waited for; matrix products, arithmetic and copies ran while one was open for 0% of the time, Pallas kernels for 0%

profile of v1, /device:TPU:1, one launch (start us, length us, event | category | flops | bytes accessed | tf_op | source)
XLA Modules:
  0.0 1617.9 jit_solution(11650293335633039890)
XLA Ops:
  10.2 1002.1 %while.16 = (s32[]{:T(128)}, f32[1024,512]{1,0:T(8,128)S(1)}, s32[128,1024]{1,0:T(8,128)}, f32[128]{0:T(128)S(1)}, f32[1024]{0:T(1024)S(1)}, /*index=5*/s32[]{:T...) while((s32[]{:T(128)}, f32[1024,512]{1,0:T(8,128)S(1)}, ...), condition=%wide.region_2.3_spmd.clone, body=%wide.region_0.2_spmd.clone.sunk | while | flops 18415628 | bytes 8573421 | solution.py:48
  11.0 129.6 %all-gather.6.cloned.1.call-done = bf16[1024,512]{1,0:T(8,128)(2,1)} async-done(((bf16[16,512]{1,0:T(8,128)(2,1)}), bf16[1024,512]{1,0:T(8,128)(2,1)}) %all-gather.6.cloned.1.call-update) | async-done | bytes 1048592 | tf_op jit(solution)/shard_map/while/body/eval_jaxpr/all_gather | solution.py:9
  140.6 1.4 reduce_sum.16
  142.0 1.6 select_add_fusion.2
  144.4 120.4 %all-gather.6.cloned.1.call-done = bf16[1024,512]{1,0:T(8,128)(2,1)} async-done(((bf16[16,512]{1,0:T(8,128)(2,1)}), bf16[1024,512]{1,0:T(8,128)(2,1)}) %all-gather.6.cloned.1.call-update) | async-done | bytes 1048592 | tf_op jit(solution)/shard_map/while/body/eval_jaxpr/all_gather | solution.py:9
  264.9 1.4 reduce_sum.16
  266.3 1.6 select_add_fusion.2
  268.7 120.4 %all-gather.6.cloned.1.call-done = bf16[1024,512]{1,0:T(8,128)(2,1)} async-done(((bf16[16,512]{1,0:T(8,128)(2,1)}), bf16[1024,512]{1,0:T(8,128)(2,1)}) %all-gather.6.cloned.1.call-update) | async-done | bytes 1048592 | tf_op jit(solution)/shard_map/while/body/eval_jaxpr/all_gather | solution.py:9
  389.1 1.4 reduce_sum.16
  390.5 1.6 select_add_fusion.2
  392.8 120.2 %all-gather.6.cloned.1.call-done = bf16[1024,512]{1,0:T(8,128)(2,1)} async-done(((bf16[16,512]{1,0:T(8,128)(2,1)}), bf16[1024,512]{1,0:T(8,128)(2,1)}) %all-gather.6.cloned.1.call-update) | async-done | bytes 1048592 | tf_op jit(solution)/shard_map/while/body/eval_jaxpr/all_gather | solution.py:9
  513.0 1.4 reduce_sum.16
  514.4 1.6 select_add_fusion.2
  516.8 120.2 %all-gather.6.cloned.1.call-done = bf16[1024,512]{1,0:T(8,128)(2,1)} async-done(((bf16[16,512]{1,0:T(8,128)(2,1)}), bf16[1024,512]{1,0:T(8,128)(2,1)}) %all-gather.6.cloned.1.call-update) | async-done | bytes 1048592 | tf_op jit(solution)/shard_map/while/body/eval_jaxpr/all_gather | solution.py:9
  636.9 1.4 reduce_sum.16
  638.3 1.6 select_add_fusion.2
  640.7 120.2 %all-gather.6.cloned.1.call-done = bf16[1024,512]{1,0:T(8,128)(2,1)} async-done(((bf16[16,512]{1,0:T(8,128)(2,1)}), bf16[1024,512]{1,0:T(8,128)(2,1)}) %all-gather.6.cloned.1.call-update) | async-done | bytes 1048592 | tf_op jit(solution)/shard_map/while/body/eval_jaxpr/all_gather | solution.py:9
  760.8 1.4 reduce_sum.16
  762.2 1.6 select_add_fusion.2
  764.7 120.4 %all-gather.6.cloned.1.call-done = bf16[1024,512]{1,0:T(8,128)(2,1)} async-done(((bf16[16,512]{1,0:T(8,128)(2,1)}), bf16[1024,512]{1,0:T(8,128)(2,1)}) %all-gather.6.cloned.1.call-update) | async-done | bytes 1048592 | tf_op jit(solution)/shard_map/while/body/eval_jaxpr/all_gather | solution.py:9
  885.1 1.4 reduce_sum.16
  886.5 1.6 select_add_fusion.2
  888.9 120.4 %all-gather.6.cloned.1.call-done = bf16[1024,512]{1,0:T(8,128)(2,1)} async-done(((bf16[16,512]{1,0:T(8,128)(2,1)}), bf16[1024,512]{1,0:T(8,128)(2,1)}) %all-gather.6.cloned.1.call-update) | async-done | bytes 1048592 | tf_op jit(solution)/shard_map/while/body/eval_jaxpr/all_gather | solution.py:9
  1009.3 1.4 reduce_sum.16
  1010.7 1.6 select_add_fusion.2
  1012.4 1.3 copy-done.1
  1013.7 89.9 %reduce-scatter.5.cloned.1.call-done = f32[128,512]{1,0:T(8,128)} async-done(((f32[1024,512]{1,0:T(8,128)}), f32[128,512]{1,0:T(8,128)}) %reduce-scatter.5.cloned.1.call-update) | async-done | bytes 262160 | tf_op jit(solution)/shard_map/reduce_scatter | solution.py:51
  1104.8 1.3 fusion.3
  1106.2 1.3 copy.11
  1107.6 86.7 %reduce-scatter.7.cloned.1.call-done = f32[64,512]{1,0:T(8,128)} async-done(((f32[512,512]{1,0:T(8,128)}), f32[64,512]{1,0:T(8,128)}) %reduce-scatter.7.cloned.1.call-update) | async-done | bytes 131088
  1194.3 1.7 copy.12
  1197.1 411.5 %all-reduce.2.cloned.1.call-done = f32[64,512]{0,1:T(8,128)} async-done(((f32[64,512]{0,1:T(8,128)}), f32[64,512]{0,1:T(8,128)}) %all-reduce.2.cloned.1.call-update) | async-done | bytes 131088 | tf_op jit(solution)/shard_map/psum | solution.py:60
  (53 shorter events, 12.6 us)
Async XLA Ops:
  8.0 1188.1 %copy-start = (bf16[512,512]{1,0:T(8,128)(2,1)S(1)}, bf16[512,512]{1,0:T(8,128)(2,1)}, u32[]{:S(2)}) copy-start(bf16[512,512]{1,0:T(8,128)(2,1)} %param.15) | copy-start | bytes 1572868
  10.2 130.4 %all-gather.6.cloned.1.call-start = ((), (), s32[]{:S(2)}) async-start(), calls=%async_computation.5 | async-start | bytes 1064960 | tf_op jit(solution)/shard_map/while/body/eval_jaxpr/all_gather | solution.py:9
  143.6 121.3 %all-gather.6.cloned.1.call-start = ((), (), s32[]{:S(2)}) async-start(), calls=%async_computation.5 | async-start | bytes 1064960 | tf_op jit(solution)/shard_map/while/body/eval_jaxpr/all_gather | solution.py:9
  267.8 121.2 %all-gather.6.cloned.1.call-start = ((), (), s32[]{:S(2)}) async-start(), calls=%async_computation.5 | async-start | bytes 1064960 | tf_op jit(solution)/shard_map/while/body/eval_jaxpr/all_gather | solution.py:9
  392.1 120.9 %all-gather.6.cloned.1.call-start = ((), (), s32[]{:S(2)}) async-start(), calls=%async_computation.5 | async-start | bytes 1064960 | tf_op jit(solution)/shard_map/while/body/eval_jaxpr/all_gather | solution.py:9
  516.0 120.9 %all-gather.6.cloned.1.call-start = ((), (), s32[]{:S(2)}) async-start(), calls=%async_computation.5 | async-start | bytes 1064960 | tf_op jit(solution)/shard_map/while/body/eval_jaxpr/all_gather | solution.py:9
  639.9 120.9 %all-gather.6.cloned.1.call-start = ((), (), s32[]{:S(2)}) async-start(), calls=%async_computation.5 | async-start | bytes 1064960 | tf_op jit(solution)/shard_map/while/body/eval_jaxpr/all_gather | solution.py:9
  763.8 121.3 %all-gather.6.cloned.1.call-start = ((), (), s32[]{:S(2)}) async-start(), calls=%async_computation.5 | async-start | bytes 1064960 | tf_op jit(solution)/shard_map/while/body/eval_jaxpr/all_gather | solution.py:9
  888.1 121.3 %all-gather.6.cloned.1.call-start = ((), (), s32[]{:S(2)}) async-start(), calls=%async_computation.5 | async-start | bytes 1064960 | tf_op jit(solution)/shard_map/while/body/eval_jaxpr/all_gather | solution.py:9
  1012.3 1.3 copy-start.1
  1012.3 91.3 %copy-start.3 = (bf16[128,512]{1,0:T(8,128)(2,1)S(1)}, bf16[128,512]{1,0:T(8,128)(2,1)}, u32[]{:S(2)}) copy-start(bf16[128,512]{1,0:T(8,128)(2,1)} %param.14) | copy-start | bytes 393220
  1012.3 91.3 %reduce-scatter.5.cloned.1.call-start = ((), (), s32[]{:S(2)}) async-start(), calls=%async_computation.2 | async-start | bytes 2359296 | tf_op jit(solution)/shard_map/reduce_scatter | solution.py:51
  1013.7 180.7 %reduce-scatter.7.cloned.1.call-start = ((), (), s32[]{:S(2)}) async-start(), calls=%async_computation.4 | async-start | bytes 1179648
  1106.2 89.9 %copy-start.2 = (f32[128,512]{1,0:T(8,128)S(1)}, f32[128,512]{1,0:T(8,128)}, u32[]{:S(2)}) copy-start(f32[128,512]{1,0:T(8,128)} %reduce-scatter.5.cloned.1.call-done) | copy-start | bytes 786436
  1107.5 501.0 %all-reduce.2.cloned.1.call-start = ((), (), s32[]{:S(2)}) async-start(), calls=%async_computation.3 | async-start | bytes 524288 | tf_op jit(solution)/shard_map/psum | solution.py:60
Sparse Core Ops, SparseCore 0:
  13.8 126.8 all-gather.5
  147.1 117.6 all-gather.5
  271.4 117.6 all-gather.5
  395.3 117.6 all-gather.5
  519.2 117.6 all-gather.5
  643.1 117.6 all-gather.5
  767.4 117.6 all-gather.5
  891.6 117.6 all-gather.5
Sparse Core Ops, SparseCore 1:
  1017.4 86.1 reduce-scatter.4
  1107.9 86.4 reduce-scatter.6
  1197.1 411.4 all-reduce.1
